TPU v7x, 512 devices: a whole 4x4x16 slice. The times are simulated.
512 devices in a mesh: wide: 64 (over x, z), narrow: 8 (over y, core).
Axes of the slice: x: 4, y: 4, z: 16, core: 2. Of those that a mesh axis runs over, the one named last changes fastest.
Arguments:
- tokens: bfloat16 [4096, 2, 5120], P('wide', None, 'narrow'), may hold values from -6 to 6
- qkv_weight: bfloat16 [5120, 6144], P('wide', 'narrow'), may hold values from -0.078125 to 0.078125
- rotated_prefix_keys: bfloat16 [64, 2048, 1024], P('wide', None, 'narrow'), may hold values from -120 to 120
- shared_prefix_values: bfloat16 [64, 2048, 1024], P('wide', None, 'narrow'), may hold values from -6 to 6
- prefix_of: int32 [4096, 1], P('wide'), may hold values from 0 to 63; in each aligned block of 64 rows (0 to 63, 64 to 127, ...) at most 2 rows name the same one
- positions: int32 [4096], P('wide'), may hold values from 512 to 2048, as said below
Outputs:
- attended: bfloat16 [4096, 2, 4096], P('wide', None, 'narrow')
Inputs may be any that keep to these rules, and one draw needn't show every extreme that they name: `prefix_of`: the 64 requests of one index of wide name each prefix at most 2 times, a bound that some block reaches. The new tokens of request r sit at positions[r] + s.
All inputs are finite; a program needn't handle non-finite values.
Results may differ from a plain program's by a relative error of at most 0.012.
The roundings to bfloat16 on the way count: a program that leaves them out, or rounds other values in their place, can miss the bound.
Values may be sent and summed in bfloat16 or wider, within the bound.
A program may use at most 64 MiB of HBM per device.

v0:
```python
import jax
import jax.numpy as jnp
from jax import lax
from jax.sharding import PartitionSpec as P

QUERY_HEADS = 32
KEY_VALUE_HEADS = 8
HEAD_SIZE = 128
DECODE_STEPS = 2


def rotate(value_block, where):
    half = HEAD_SIZE // 2
    freq = 10000.0 ** (-(jnp.arange(half, dtype=jnp.float32) * 2.0 / HEAD_SIZE))
    angle = where[..., None].astype(jnp.float32) * freq
    cosine = jnp.cos(angle)
    sine = jnp.sin(angle)
    first_index = value_block[..., :half]
    second = value_block[..., half:]
    return jnp.concatenate(
        [first_index * cosine - second * sine, second * cosine + first_index * sine], axis=-1
    )


def prefix_part(asked, bounds, key_rows, value_block):
    scale = 1.0 / HEAD_SIZE**0.5
    far = (
        jnp.einsum("nskgd,lkd->nskgl", asked, key_rows, preferred_element_type=jnp.float32) * scale
    )
    allowed = jnp.arange(key_rows.shape[0], dtype=jnp.int32)[None, :] < bounds[:, None]
    far = jnp.where(allowed[:, None, None, None, :], far, -1e30)
    top = jnp.max(far, axis=-1)
    weight = jnp.exp(far - top[..., None])
    total = jnp.sum(weight, axis=-1)
    summed = jnp.einsum(
        "nskgl,lkd->nskgd",
        weight.astype(jnp.bfloat16),
        value_block,
        preferred_element_type=jnp.float32,
    )
    return (summed, top, total)


def own_part(asked, near_keys, near_values):
    scale = 1.0 / HEAD_SIZE**0.5
    near = (
        jnp.einsum("nskgd,ntkd->nskgt", asked, near_keys, preferred_element_type=jnp.float32)
        * scale
    )
    causal = jnp.arange(DECODE_STEPS)[:, None] >= jnp.arange(DECODE_STEPS)[None, :]
    near = jnp.where(causal[None, :, None, None, :], near, -1e30)
    top = jnp.max(near, axis=-1)
    weight = jnp.exp(near - top[..., None])
    total = jnp.sum(weight, axis=-1)
    summed = jnp.einsum(
        "nskgt,ntkd->nskgd",
        weight.astype(jnp.bfloat16),
        near_values,
        preferred_element_type=jnp.float32,
    )
    return (summed, top, total)


def combine(first_index, second):
    top = jnp.maximum(first_index[1], second[1])
    left = jnp.exp(first_index[1] - top)
    right = jnp.exp(second[1] - top)
    summed = first_index[0] * left[..., None] + second[0] * right[..., None]
    return (summed, top, first_index[2] * left + second[2] * right)


def fold_rows(inputs, piece):
    return jnp.dot(inputs, piece, preferred_element_type=jnp.float32)


def on_device(tokens, qkv_weight, rotated_prefix_keys, shared_prefix_values, prefix_of, positions):
    rows_dev = tokens.shape[0]
    owners = lax.axis_size("wide")
    capacity = max(2, (2 * rows_dev + owners - 1) // owners)
    kv_local = rotated_prefix_keys.shape[2] // HEAD_SIZE
    query_group = QUERY_HEADS // KEY_VALUE_HEADS
    whole = lax.all_gather(tokens, "narrow", axis=2, tiled=True)
    inputs = whole.reshape(rows_dev * DECODE_STEPS, whole.shape[2])
    mixed_output = fold_rows(inputs, lax.all_gather(qkv_weight, "wide", axis=0, tiled=True))
    mixed_output = mixed_output.reshape(
        rows_dev, DECODE_STEPS, kv_local, query_group + 2, HEAD_SIZE
    )
    where = positions[:, None] + jnp.arange(DECODE_STEPS, dtype=jnp.int32)[None, :]
    query = rotate(mixed_output[:, :, :, :query_group, :], where[:, :, None, None]).astype(
        jnp.bfloat16
    )
    own_key = rotate(mixed_output[:, :, :, query_group, :], where[:, :, None]).astype(jnp.bfloat16)
    own_value = mixed_output[:, :, :, query_group + 1, :].astype(jnp.bfloat16)
    chosen_prefix = prefix_of[:, 0]
    hits = (chosen_prefix[:, None] == jnp.arange(owners, dtype=jnp.int32)[None, :]).astype(
        jnp.int32
    )
    rank = jnp.sum((jnp.cumsum(hits, axis=0) - hits) * hits, axis=1)
    target = chosen_prefix * capacity + rank
    slots = owners * capacity
    dispatch = target[None, :] == jnp.arange(slots, dtype=jnp.int32)[:, None]
    route = dispatch.astype(jnp.bfloat16)
    limits = jnp.sum(jnp.where(dispatch, positions[None, :], 0), axis=1).reshape(owners, capacity)
    key_rows = rotated_prefix_keys[0].reshape(-1, kv_local, HEAD_SIZE)
    value_block = shared_prefix_values[0].reshape(-1, kv_local, HEAD_SIZE)
    flat = query.reshape(rows_dev, -1)
    packed = jnp.dot(route, flat, preferred_element_type=jnp.float32).astype(jnp.bfloat16)
    asked = lax.all_to_all(
        packed.reshape(owners, capacity, flat.shape[1]),
        "wide",
        split_axis=0,
        concat_axis=0,
        tiled=True,
    )
    bounds = lax.all_to_all(limits, "wide", split_axis=0, concat_axis=0, tiled=True)
    count = asked.shape[1]
    items = owners * count
    summed, top, total = prefix_part(
        asked.reshape(items, DECODE_STEPS, kv_local, query_group, HEAD_SIZE),
        bounds.reshape(items),
        key_rows,
        value_block,
    )
    summed, top, total = (
        lax.all_to_all(
            summed.reshape(owners, count, -1).astype(jnp.bfloat16),
            "wide",
            split_axis=0,
            concat_axis=0,
            tiled=True,
        ).astype(jnp.float32),
        lax.all_to_all(
            top.reshape(owners, count, -1).astype(jnp.bfloat16),
            "wide",
            split_axis=0,
            concat_axis=0,
            tiled=True,
        ).astype(jnp.float32),
        lax.all_to_all(
            total.reshape(owners, count, -1).astype(jnp.bfloat16),
            "wide",
            split_axis=0,
            concat_axis=0,
            tiled=True,
        ).astype(jnp.float32),
    )
    far = (
        jnp.take(summed.reshape(slots, -1), target, axis=0).reshape(
            rows_dev, DECODE_STEPS, kv_local, query_group, HEAD_SIZE
        ),
        jnp.take(top.reshape(slots, -1), target, axis=0).reshape(
            rows_dev, DECODE_STEPS, kv_local, query_group
        ),
        jnp.take(total.reshape(slots, -1), target, axis=0).reshape(
            rows_dev, DECODE_STEPS, kv_local, query_group
        ),
    )
    near = own_part(query, own_key, own_value)
    merged, merged_top, merged_total = combine(far, near)
    result = merged / merged_total[..., None]
    return result.astype(jnp.bfloat16).reshape(
        rows_dev, DECODE_STEPS, kv_local * query_group * HEAD_SIZE
    )


def solution(mesh):
    return jax.shard_map(
        on_device,
        mesh=mesh,
        in_specs=(
            P("wide", None, "narrow"),
            P("wide", "narrow"),
            P("wide", None, "narrow"),
            P("wide", None, "narrow"),
            P("wide", None),
            P("wide"),
        ),
        out_specs=P("wide", None, "narrow"),
        check_vma=False,
    )
```

profile of v0, /device:TPU:1, one launch (start us, length us, event | category | flops | bytes accessed | tf_op | source)
XLA Modules:
  0.0 324.1 jit_solution(3295242763182676038)
XLA Ops:
  6.5 0.7 all-gather.5.cloned.1.call-update
  7.3 1.6 copy.61
  8.9 0.7 fusion.45
  9.7 0.8 select_reduce_fusion.1
  10.6 0.7 compare_and_fusion
  11.3 0.7 select_reduce_fusion
  12.0 0.8 all_to_all.18
  12.8 19.1 %all-to-all-start = ((s32[64,1,2]{2,1,0:T(1,128)}), s32[64,1,2]{2,1,0:T(1,128)S(1)}, u32[]{:S(2)}, u32[]{:S(2)}) async-start(s32[64,1,2]{2,1,0:T(1,128)} %bitcast.3), calls=%async_computation | async-start | bytes 65536 | tf_op jit(solution)/shard_map/all_to_all | solution.py:115
  31.9 0.7 and_bitcast_fusion
  32.6 0.7 add_convert_fusion.1
  33.3 0.3 multiply_cosine_fusion.1
  33.6 11.6 %all-to-all-done = s32[64,1,2]{2,1,0:T(1,128)S(1)} async-done(((s32[64,1,2]{2,1,0:T(1,128)}), s32[64,1,2]{2,1,0:T(1,128)S(1)}, u32[]{:S(2)}, u32[]{:S(2)}) %all-to-all-start) | async-done | bytes 544 | tf_op jit(solution)/shard_map/all_to_all | solution.py:115
  45.1 0.5 broadcast.198
  45.6 0.7 reduce.7
  46.5 116.2 %all-gather.5.cloned.1.call-done = bf16[5120,768]{1,0:T(8,128)(2,1)} async-done(((bf16[80,768]{1,0:T(8,128)(2,1)}), bf16[5120,768]{1,0:T(8,128)(2,1)}) %all-gather.5.cloned.1.call-update) | async-done | bytes 7864336 | tf_op jit(solution)/shard_map/all_gather | solution.py:84
  162.8 10.6 %copy.62 = bf16[768,5120]{1,0:T(8,128)(2,1)} copy(bf16[768,5120]{0,1:T(8,128)(2,1)} %bitcast.138) | data formatting | bytes 15728640 | tf_op jit(solution)/shard_map/dot_general | solution.py:73
  173.3 26.7 %all-gather.3.cloned.1.call-done = bf16[64,2,5120]{2,0,1:T(8,128)(2,1)} async-done(((bf16[64,2,640]{2,0,1:T(8,128)(2,1)}), bf16[64,2,5120]{2,0,1:T(8,128)(2,1)}) %all-gather.3.cloned.1.call-update) | async-done | bytes 1310736 | tf_op jit(solution)/shard_map/all_gather | solution.py:82
  200.0 6.3 %fusion.9 = f32[64,2,1,6,128]{4,0,3,1,2:T(8,128)S(1)} fusion(bf16[6,128,5120,1]{2,1,0,3:T(8,128)(2,1)} %bitcast.137, bf16[64,2,5120]{2,0,1:T(8,128)(2,1)} %all-gather.3.cloned.1.call-done), kind=kOutput, calls=%fused_computation.13 | convolution fusion | flops 1006632960 | bytes 9568256 | tf_op jit(solution)/shard_map/dot_general | solution.py:73
  206.4 0.2 subtract_convert_fusion
  206.8 0.3 convolution_convert_fusion
  207.2 0.8 reshape.360
  208.0 15.3 %all-to-all-start.1 = ((bf16[64,2,1024]{2,1,0:T(2,128)(2,1)}), bf16[64,2,1024]{2,1,0:T(2,128)(2,1)S(1)}, u32[]{:S(2)}, u32[]{:S(2)}) async-start(bf16[64,2,1024]{2,1,0:T(2,128)(2,1)} %reshape.360), calls=%async_computation.1 | async-start | bytes 524288 | tf_op jit(solution)/shard_map/all_to_all | solution.py:108
  223.2 0.2 iota_compare_fusion
  223.5 0.3 fusion.47
  224.0 19.2 %all-to-all-done.1 = bf16[64,2,1024]{2,1,0:T(2,128)(2,1)S(1)} async-done(((bf16[64,2,1024]{2,1,0:T(2,128)(2,1)}), bf16[64,2,1024]{2,1,0:T(2,128)(2,1)S(1)}, u32[]{:S(2)}, u32[]{:S(2)}) %all-to-all-start.1) | async-done | bytes 262176 | tf_op jit(solution)/shard_map/all_to_all | solution.py:108
  243.2 0.2 reshape.361
  243.4 4.8 %fusion.2 = (f32[128,2,4]{0,2,1:T(4,128)S(1)}, f32[128,2,4,2048]{3,0,2,1:T(8,128)}) fusion(pred[128,2048]{1,0:T(8,128)(4,1)S(1)} %iota_compare_fusion, bf16[1,2048,128]{2,1,0:T(8,128)(2,1)S(1)} %copy-done, bf16[128,2,4,128]{3,2,1,0:T(4,128)(2,1)S(1)} %reshape.361), kind=kOutput, calls=%fused_computation.7 | convolution fusion | flops 543161344 | bytes 9441280 | tf_op jit(solution)/shard_map/nskgd,lkd->nskgl/dot_general | solution.py:28
  248.2 0.1 copy.66
  248.4 0.7 convert_element_type.90
  249.1 6.8 %all-to-all-start.3 = ((bf16[64,2,8]{2,1,0:T(2,128)(2,1)}), bf16[64,2,8]{2,1,0:T(2,128)(2,1)S(1)}, u32[]{:S(2)}, u32[]{:S(2)}) async-start(bf16[64,2,8]{2,1,0:T(2,128)(2,1)} %convert_element_type.90), calls=%async_computation.3 | async-start | bytes 65536 | tf_op jit(solution)/shard_map/all_to_all | solution.py:132
  255.9 4.6 %fusion = bf16[128,2,4]{0,2,1:T(4,128)(2,1)S(1)} fusion(f32[128,2,4,2048]{3,0,2,1:T(8,128)} %get-tuple-element.22, f32[128,2,4]{0,2,1:T(4,128)S(1)} %get-tuple-element.21, pred[128,2048]{1,0:T(8,128)(4,1)S(1)} %iota_compare_fusion), kind=kLoop, calls=%fused_computation.5 | loop fusion | flops 8387584 | bytes 8656896 | tf_op jit(solution)/shard_map/reduce_sum | solution.py:34
  260.5 0.1 copy.75
  260.6 0.7 convert_element_type.94
  261.3 7.8 %all-to-all-done.3 = bf16[64,2,8]{2,1,0:T(2,128)(2,1)S(1)} async-done(((bf16[64,2,8]{2,1,0:T(2,128)(2,1)}), bf16[64,2,8]{2,1,0:T(2,128)(2,1)S(1)}, u32[]{:S(2)}, u32[]{:S(2)}) %all-to-all-start.3) | async-done | bytes 2080 | tf_op jit(solution)/shard_map/all_to_all | solution.py:132
  269.2 6.9 %all-to-all-start.4 = ((bf16[64,2,8]{2,1,0:T(2,128)(2,1)}), bf16[64,2,8]{2,1,0:T(2,128)(2,1)S(1)}, u32[]{:S(2)}, u32[]{:S(2)}) async-start(bf16[64,2,8]{2,1,0:T(2,128)(2,1)} %convert_element_type.94), calls=%async_computation.4 | async-start | bytes 65536 | tf_op jit(solution)/shard_map/all_to_all | solution.py:139
  276.1 5.4 %fusion.15 = bf16[128,2,1,4,128]{4,0,3,1,2:T(8,128)(2,1)S(1)} fusion(f32[128,2,4,2048]{3,0,2,1:T(8,128)} %get-tuple-element.22, f32[128,2,4]{0,2,1:T(4,128)S(1)} %get-tuple-element.21, pred[128,2048]{1,0:T(8,128)(4,1)S(1)} %iota_compare_fusion, bf16[1,2048,128]{2,1,0:T(8,128)(2,1)S(1)} %copy-done.1), kind=kOutput, calls=%fused_computation.16 | convolution fusion | flops 545390592 | bytes 9441280 | tf_op jit(solution)/shard_map/nskgl,lkd->nskgd/dot_general | solution.py:35
  281.5 0.2 copy.65
  281.7 0.8 convert_element_type.88
  282.5 6.6 %all-to-all-done.4 = bf16[64,2,8]{2,1,0:T(2,128)(2,1)S(1)} async-done(((bf16[64,2,8]{2,1,0:T(2,128)(2,1)}), bf16[64,2,8]{2,1,0:T(2,128)(2,1)S(1)}, u32[]{:S(2)}, u32[]{:S(2)}) %all-to-all-start.4) | async-done | bytes 2080 | tf_op jit(solution)/shard_map/all_to_all | solution.py:139
  289.1 7.8 %all-to-all-start.2 = ((bf16[64,2,1024]{2,1,0:T(2,128)(2,1)}), bf16[64,2,1024]{2,1,0:T(2,128)(2,1)S(1)}, u32[]{:S(2)}, u32[]{:S(2)}) async-start(bf16[64,2,1024]{2,1,0:T(2,128)(2,1)} %convert_element_type.88), calls=%async_computation.2 | async-start | bytes 524288 | tf_op jit(solution)/shard_map/all_to_all | solution.py:125
  296.9 1.3 fusion.56
  298.3 0.3 fusion.34
  298.7 0.6 gather_fusion.1
  299.3 0.6 gather_fusion.2
  300.5 14.2 %all-to-all-done.2 = bf16[64,2,1024]{2,1,0:T(2,128)(2,1)S(1)} async-done(((bf16[64,2,1024]{2,1,0:T(2,128)(2,1)}), bf16[64,2,1024]{2,1,0:T(2,128)(2,1)S(1)}, u32[]{:S(2)}, u32[]{:S(2)}) %all-to-all-start.2) | async-done | bytes 262176 | tf_op jit(solution)/shard_map/all_to_all | solution.py:125
  314.8 0.7 gather_fusion
  315.6 1.0 fusion.22
  316.6 0.7 reshape.374
  (35 shorter events, 1.8 us)
Async XLA Ops:
  6.5 236.9 %copy-start = (bf16[1,2048,128]{2,1,0:T(8,128)(2,1)S(1)}, bf16[1,2048,128]{2,1,0:T(8,128)(2,1)}, u32[]{:S(2)}) copy-start(bf16[1,2048,128]{2,1,0:T(8,128)(2,1)} %param.10) | copy-start | bytes 1572868
  6.5 156.2 %all-gather.5.cloned.1.call-start = ((), (), s32[]{:S(2)}) async-start(), calls=%async_computation.6 | async-start | bytes 7987200 | tf_op jit(solution)/shard_map/all_gather | solution.py:84
  7.3 192.8 %all-gather.3.cloned.1.call-start = ((), (), s32[]{:S(2)}) async-start(), calls=%async_computation.5 | async-start | bytes 1474560 | tf_op jit(solution)/shard_map/all_gather | solution.py:82
  12.8 32.4 %all-to-all-start = ((s32[64,1,2]{2,1,0:T(1,128)}), s32[64,1,2]{2,1,0:T(1,128)S(1)}, u32[]{:S(2)}, u32[]{:S(2)}) async-start(s32[64,1,2]{2,1,0:T(1,128)} %bitcast.3), calls=%async_computation | async-start | bytes 65536 | tf_op jit(solution)/shard_map/all_to_all | solution.py:115
  208.0 35.2 %all-to-all-start.1 = ((bf16[64,2,1024]{2,1,0:T(2,128)(2,1)}), bf16[64,2,1024]{2,1,0:T(2,128)(2,1)S(1)}, u32[]{:S(2)}, u32[]{:S(2)}) async-start(bf16[64,2,1024]{2,1,0:T(2,128)(2,1)} %reshape.360), calls=%async_computation.1 | async-start | bytes 524288 | tf_op jit(solution)/shard_map/all_to_all | solution.py:108
  243.4 32.7 %copy-start.1 = (bf16[1,2048,128]{2,1,0:T(8,128)(2,1)S(1)}, bf16[1,2048,128]{2,1,0:T(8,128)(2,1)}, u32[]{:S(2)}) copy-start(bf16[1,2048,128]{2,1,0:T(8,128)(2,1)} %param.11) | copy-start | bytes 1572868
  249.1 20.1 %all-to-all-start.3 = ((bf16[64,2,8]{2,1,0:T(2,128)(2,1)}), bf16[64,2,8]{2,1,0:T(2,128)(2,1)S(1)}, u32[]{:S(2)}, u32[]{:S(2)}) async-start(bf16[64,2,8]{2,1,0:T(2,128)(2,1)} %convert_element_type.90), calls=%async_computation.3 | async-start | bytes 65536 | tf_op jit(solution)/shard_map/all_to_all | solution.py:132
  269.2 19.9 %all-to-all-start.4 = ((bf16[64,2,8]{2,1,0:T(2,128)(2,1)}), bf16[64,2,8]{2,1,0:T(2,128)(2,1)S(1)}, u32[]{:S(2)}, u32[]{:S(2)}) async-start(bf16[64,2,8]{2,1,0:T(2,128)(2,1)} %convert_element_type.94), calls=%async_computation.4 | async-start | bytes 65536 | tf_op jit(solution)/shard_map/all_to_all | solution.py:139
  289.1 25.6 %all-to-all-start.2 = ((bf16[64,2,1024]{2,1,0:T(2,128)(2,1)}), bf16[64,2,1024]{2,1,0:T(2,128)(2,1)S(1)}, u32[]{:S(2)}, u32[]{:S(2)}) async-start(bf16[64,2,1024]{2,1,0:T(2,128)(2,1)} %convert_element_type.88), calls=%async_computation.2 | async-start | bytes 524288 | tf_op jit(solution)/shard_map/all_to_all | solution.py:125
Sparse Core Ops, SparseCore 0:
  10.3 152.4 all-gather.4
  164.9 35.1 all-gather.2
where the time goes:
time: 328 us; the launch traced here: 324 us
  waiting for transfers between devices  203 us (62%)
  starting transfers between devices  55.9 us (17%)
  local copies, waits for them, and re-layouts  20.9 us (6%)
  matrix products  19.2 us (6%)
  between operations  13.7 us (4%)
  other arithmetic  11.4 us (3%)
    all_gather x1, waiting for transfers between devices, on_device(): lax.all_gather(qkv_weight, 'wide', axis=0, tiled=True)  116 us
    all_gather x1, waiting for transfers between devices, on_device(): whole = lax.all_gather(tokens, 'narrow', axis=2, tiled=True)  26.7 us
    all_to_all x1, waiting for transfers between devices, on_device(): lax.all_to_all(packed.reshape(owners, capacity, flat.shape[1]), 'wide', s...  19.2 us
    all_to_all x1, starting transfers between devices, on_device(): lax.all_to_all(limits, 'wide', split_axis=0, concat_axis=0, tiled=True)  19.1 us
    all_to_all x1, starting transfers between devices, on_device(): lax.all_to_all(packed.reshape(owners, capacity, flat.shape[1]), 'wide', s...  15.3 us
    all_to_all x1, waiting for transfers between devices, on_device(): lax.all_to_all(summed.reshape(owners, count, -1).astype(jnp.bfloat16), 'w...  14.2 us
    all_to_all x1, waiting for transfers between devices, on_device(): lax.all_to_all(limits, 'wide', split_axis=0, concat_axis=0, tiled=True)  11.6 us
    dot_general x1, local copies, waits for them, and re-layouts, fold_rows(): return jnp.dot(inputs, piece, preferred_element_type=jnp.float32)  10.6 us
  transfers between devices with their start and end apart: 7, of which 7 were waited for; matrix products, arithmetic and copies ran while one was open for 11% of the time, Pallas kernels for 0%

commit v1 on v0

v1 whole, which is shorter than its diff:
```python
import functools
import math

import jax
import jax.numpy as jnp
from jax import lax
from jax.experimental import pallas as pl
from jax.experimental.pallas import tpu as pltpu
from jax.sharding import PartitionSpec as P

HEAD = 128
STEPS = 2
XS = 4
MESH = pl.DeviceIdType.MESH
BF = jnp.bfloat16
F32 = jnp.float32
I32 = jnp.int32
HI = lax.Precision.HIGHEST


def iota(shape, dim):
    return lax.broadcasted_iota(I32, shape, dim)


def to_column(row, n):
    eye = iota((n, row.shape[1]), 0) == iota((n, row.shape[1]), 1)
    return jnp.sum(jnp.where(eye, row, 0), axis=1, keepdims=True)


def frequencies():
    lane = iota((1, HEAD), 1) % (HEAD // 2)
    high, low = lane // 8, lane % 8
    a = jnp.full((1, HEAD), 1.0, F32)
    b = jnp.full((1, HEAD), 1.0, F32)
    for t in range(1, 8):
        a = jnp.where(high == t, 10000.0 ** (-8 * t / 64), a)
        b = jnp.where(low == t, 10000.0 ** (-t / 64), b)
    return a * b


def kernel(
    dims,
    tok,
    w,
    keys,
    vals,
    pref,
    pos,
    out,
    wbuf,
    tokbuf,
    kbuf,
    vbuf,
    meta,
    metabuf,
    cosbuf,
    sinbuf,
    limsend,
    limrecv,
    hsend,
    hrecv,
    qsend,
    qrecv,
    fsend,
    frecv,
    lsend,
    lrecv,
    wxs,
    wxr,
    zs,
    zr,
    ps,
    pr,
    t1s,
    t1r,
    m1s,
    m1r,
    ys,
    yr,
    kvs,
    hs,
    hr,
    ais,
    air,
    loc,
):
    zn, yn = dims
    pn = XS * zn
    t_rows = tok.shape[0]
    reqs = t_rows // STEPS
    wide, nar = lax.axis_index("wide"), lax.axis_index("narrow")
    x, z = wide // zn, wide % zn
    y, c = nar // 2, nar % 2
    k, jx = x // 2, x % 2
    selfcase = k == c

    def dev(xx, zz, yy, cc):
        return {"wide": xx * zn + zz, "narrow": yy * 2 + cc}

    def remote(src, dst, ss, rs, where):
        return pltpu.make_async_remote_copy(
            src_ref=src, dst_ref=dst, send_sem=ss, recv_sem=rs, device_id=where, device_id_type=MESH
        )

    def took(ref, sem):
        pltpu.make_async_copy(ref, ref, sem).wait()

    up_z, down_z = (z + 1) % zn, (z + zn - 1) % zn
    up_y, down_y = (y + 1) % yn, (y + yn - 1) % yn

    barrier = pltpu.get_barrier_semaphore()
    peers = [dev((x + o) % XS, z, y, (c + d) % 2) for o in range(XS) for d in range(2) if o or d]
    if zn > 1:
        peers += [dev(x, up_z, y, c), dev(x, down_z, y, c)]
    if yn > 1:
        peers += [dev(x, z, up_y, c), dev(x, z, down_y, c)]
    for peer in peers:
        pl.semaphore_signal(barrier, inc=1, device_id=peer, device_id_type=MESH)

    kcopy = pltpu.make_async_copy(keys.at[0], kbuf, kvs.at[0])
    vcopy = pltpu.make_async_copy(vals.at[0], vbuf, kvs.at[1])
    kcopy.start()
    vcopy.start()

    pcol = to_column(pref[...], reqs)
    before = (pcol == pref[...]) & (iota((reqs, reqs), 0) < iota((reqs, reqs), 1))
    rank = jnp.sum(before.astype(I32), axis=0, keepdims=True)
    code_col = to_column(pref[...] * 8 + rank * 2, reqs)
    pos_col = to_column(pos[...], reqs)
    spread = iota((reqs, t_rows), 0) == iota((reqs, t_rows), 1) % reqs
    step_lane = iota((1, t_rows), 1) // reqs
    code_row = jnp.sum(jnp.where(spread, code_col, 0), axis=0, keepdims=True) + step_lane
    place_row = jnp.sum(jnp.where(spread, pos_col, 0), axis=0, keepdims=True) + step_lane
    which = iota((8, t_rows), 0)
    meta[...] = jnp.where(which == 0, code_row, jnp.where(which == 1, place_row, 0))

    pl.semaphore_wait(barrier, len(peers))

    def wx(j, part):
        if part == 0:
            src = w.at[:, pl.ds(2 * HEAD * j, 2 * HEAD)]
            dst = wbuf.at[wide, :, pl.ds(0, 2 * HEAD)]
        else:
            src = w.at[:, pl.ds(4 * HEAD + HEAD * j, HEAD)]
            dst = wbuf.at[wide, :, pl.ds(2 * HEAD, HEAD)]
        rsem = wxr.at[jx, part]
        return (
            remote(src, dst, wxs.at[j, part], rsem, dev(2 * c + j, z, y, k)),
            pltpu.make_async_copy(src, dst, rsem),
        )

    def either(pair, is_self):
        @pl.when(is_self)
        def _():
            pair[1].start()

        @pl.when(jnp.logical_not(is_self))
        def _():
            pair[0].start()

    def sent(pair, is_self):
        @pl.when(jnp.logical_not(is_self))
        def _():
            pair[0].wait_send()

    for j in range(2):
        for part in range(2):
            either(wx(j, part), selfcase & (jx == j))

    def tok1(o):
        target = dev((x + o) % XS, z, y, k)
        src, dst, rsem = tok, tokbuf.at[nar, jx], t1r.at[c, jx]
        return remote(src, dst, t1s.at[o], rsem, target), pltpu.make_async_copy(src, dst, rsem)

    def met1(o):
        target = dev((x + o) % XS, z, y, k)
        src, dst, rsem = meta, metabuf.at[c, jx], m1r.at[c, jx]
        return remote(src, dst, m1s.at[o], rsem, target), pltpu.make_async_copy(src, dst, rsem)

    for o in range(XS):
        either(tok1(o), selfcase if o == 0 else jnp.bool_(False)) if o == 0 else tok1(o)[0].start()
    for o in range(XS):
        either(met1(o), selfcase) if o == 0 else met1(o)[0].start()

    def reach(n):
        return {(0, 0): n // 2, (0, 1): (n - 1) // 2, (1, 0): (n - 1) // 2, (1, 1): n // 2}

    zreach, yreach = reach(zn), reach(yn)
    zto = (up_z, down_z)
    yto = (up_y, down_y)

    def zsend(direction, i, d):
        origin = (z + zn - d) % zn if direction == 0 else (z + d) % zn
        slot = (2 * c + i) * zn + origin
        remote(
            wbuf.at[slot], wbuf.at[slot], zs, zr.at[direction, i, d], dev(x, zto[direction], y, c)
        ).start()

    def partner(i, origin):
        slot = (2 * c + i) * zn + origin
        remote(wbuf.at[slot], wbuf.at[slot], ps, pr, dev(x, z, y, 1 - c)).start()

    def ysend(direction, i, cc, d):
        origin = (y + yn - d) % yn if direction == 0 else (y + d) % yn
        slot = origin * 2 + cc
        remote(
            tokbuf.at[slot, i],
            tokbuf.at[slot, i],
            ys,
            yr.at[direction, i, cc, d],
            dev(x, z, yto[direction], c),
        ).start()

    for i in range(2):
        slot = (2 * c + i) * zn + z
        took(wbuf.at[slot, :, pl.ds(0, 2 * HEAD)], wxr.at[i, 0])
        took(wbuf.at[slot, :, pl.ds(2 * HEAD, HEAD)], wxr.at[i, 1])
        for direction in range(2):
            if zreach[direction, i] > 0:
                zsend(direction, i, 0)
        partner(i, z)

    for i in range(2):
        for cc in range(2):
            took(tokbuf.at[y * 2 + cc, i], t1r.at[cc, i])
            for direction in range(2):
                if yreach[direction, i] > 0:
                    ysend(direction, i, cc, 0)

    def angles():
        freq = frequencies()
        for i in range(2):
            for cc in range(2):
                took(metabuf.at[cc, i], m1r.at[cc, i])
            place = to_column(metabuf[0, i, 1:2, :], t_rows).astype(F32)
            angle = place * freq
            low = iota((t_rows, HEAD), 1) < HEAD // 2
            sine = jnp.sin(angle)
            cosbuf[i] = jnp.cos(angle)
            sinbuf[i] = jnp.where(low, -sine, sine)

    def ystep(d):
        for i in range(2):
            for direction in range(2):
                if d <= yreach[direction, i]:
                    origin = (y + yn - d) % yn if direction == 0 else (y + d) % yn
                    for cc in range(2):
                        took(tokbuf.at[origin * 2 + cc, i], yr.at[direction, i, cc, d - 1])
                        if d < yreach[direction, i]:
                            ysend(direction, i, cc, d)

    ysteps = yn // 2
    ydone = 0
    for d in range(1, zn // 2 + 1):
        for i in range(2):
            for direction in range(2):
                if d <= zreach[direction, i]:
                    origin = (z + zn - d) % zn if direction == 0 else (z + d) % zn
                    slot = (2 * c + i) * zn + origin
                    took(wbuf.at[slot], zr.at[direction, i, d - 1])
                    if d < zreach[direction, i]:
                        zsend(direction, i, d)
                    partner(i, origin)
        if d == 1:
            angles()
        if ydone < ysteps - 1 and d == min(4, zn // 2):
            ydone += 1
            ystep(ydone)
    while ydone < ysteps:
        ydone += 1
        ystep(ydone)
    if zn < 2:
        angles()

    lane = iota((reqs, HEAD), 1)
    halves = jnp.where(lane < 4, pos_col // 64, pos_col % 64).astype(F32).astype(BF)
    code64 = pref[...] * 8 + rank * 2
    prow = iota((pn, reqs), 0) * 8
    lim = [
        jnp.dot(
            (code64 == prow + 2 * u).astype(F32).astype(BF), halves, preferred_element_type=F32
        )
        for u in range(2)
    ]
    limits = jnp.where((iota((pn, HEAD), 1) // 2) % 2 == 0, lim[0], lim[1])
    limsend[...] = limits.reshape(pn, 1, HEAD)

    took(wbuf.at[pl.ds(0, 2 * zn)], pr)

    def each_wide(fn):
        def step(o, carry):
            fn((wide + o) % pn)
            return carry

        lax.fori_loop(1, pn, step, 0)

    def send_limit(p):
        remote(
            limsend.at[p],
            limrecv.at[z * XS + x],
            ais.at[0],
            air.at[0],
            {"wide": p, "narrow": nar},
        ).start()

    each_wide(send_limit)
    own_limit = pltpu.make_async_copy(limsend.at[wide], limrecv.at[z * XS + x], loc.at[0])
    own_limit.start()

    nb = pn // (2 * yn)
    depth = w.shape[0]
    acc = None
    for n in range(2 * yn):
        left = tokbuf[n].reshape(2 * t_rows, tok.shape[1])
        right = wbuf[n * nb : (n + 1) * nb].reshape(nb * depth, 3 * HEAD)
        part = jnp.dot(left, right, preferred_element_type=F32)
        acc = part if acc is None else acc + part
    cosine = cosbuf[...].reshape(2 * t_rows, HEAD)
    sine = sinbuf[...].reshape(2 * t_rows, HEAD)

    def rotate(v):
        return v * cosine + pltpu.roll(v, HEAD // 2, 1) * sine

    q0 = rotate(acc[:, :HEAD]).astype(BF)
    q1 = rotate(acc[:, HEAD : 2 * HEAD]).astype(BF)
    third = acc[:, 2 * HEAD :]
    third = jnp.where(jx == 0, rotate(third), third).astype(BF)

    codes = jnp.concatenate([metabuf[0, i, 0:1, :] + 4 * i for i in range(2)], axis=1)
    slots = iota((8 * pn, 2 * t_rows), 0)
    onehot = (slots == codes).astype(F32).astype(BF)
    for h, q in enumerate((q0, q1)):
        packed = jnp.dot(onehot, q, preferred_element_type=F32)
        qsend[:, :, h * HEAD : (h + 1) * HEAD] = packed.reshape(pn, 8, HEAD).astype(BF)

    def send_query(p):
        remote(
            qsend.at[p], qrecv.at[z * 2 + c, jx], ais.at[1], air.at[1], {"wide": p, "narrow": y * 2 + k}
        ).start()

    each_wide(send_query)
    own_query = pltpu.make_async_copy(qsend.at[wide], qrecv.at[z * 2 + c, jx], loc.at[1])

    @pl.when(selfcase)
    def _():
        own_query.start()

    @pl.when(jnp.logical_not(selfcase))
    def _():
        send_query(wide)

    def home(i):
        src, dst, rsem = hsend.at[i], hrecv.at[jx], hr.at[jx]
        return (
            remote(src, dst, hs.at[i], rsem, dev(2 * c + i, z, y, k)),
            pltpu.make_async_copy(src, dst, rsem),
        )

    for i in range(2):
        rows = slice(i * t_rows, (i + 1) * t_rows)
        hsend[i, :, 0:HEAD] = q0[rows]
        hsend[i, :, HEAD : 2 * HEAD] = q1[rows]
        hsend[i, :, 2 * HEAD :] = third[rows]
    for i in range(2):
        either(home(i), selfcase & (jx == i))

    kcopy.wait()
    vcopy.wait()
    took(limsend.at[pl.ds(0, pn - 1)], ais.at[0])
    took(limsend.at[pl.ds(0, pn - 1)], air.at[0])
    own_limit.wait()

    rows_all = 4 * pn
    lim_rows = limrecv[...].reshape(pn, HEAD).astype(BF)
    owner = (iota((rows_all, pn), 0) // 4 == iota((rows_all, pn), 1)).astype(F32).astype(BF)
    lim_all = jnp.dot(owner, lim_rows, preferred_element_type=F32)
    rlane, rsub = iota((rows_all, HEAD), 1), iota((rows_all, HEAD), 0) % 4
    pick = jnp.where(rlane == rsub, 64.0, jnp.where(rlane == rsub + 4, 1.0, 0.0))
    limit = jnp.sum(lim_all * pick, axis=1, keepdims=True).astype(I32)

    @pl.when(selfcase)
    def _():
        own_query.wait()
        took(qsend.at[pl.ds(0, pn - 1)], ais.at[1])
        took(qsend.at[pl.ds(0, pn - 1)], air.at[1])

    @pl.when(jnp.logical_not(selfcase))
    def _():
        took(qsend, ais.at[1])
        took(qsend, air.at[1])

    scale = 1.0 / HEAD**0.5
    length = kbuf.shape[0]
    allowed = iota((rows_all, length), 1) < limit
    lse_all = jnp.zeros((rows_all, HEAD), F32)
    low8 = iota((2 * zn, 8, HEAD), 1) < 4
    for h in range(2):
        halves_out = []
        for j in range(2):
            q = qrecv[:, j, :, h * HEAD : (h + 1) * HEAD].astype(F32)
            q = q.reshape(rows_all, HEAD).astype(BF)
            s = lax.dot_general(
                q, kbuf[...], (((1,), (1,)), ((), ())), preferred_element_type=F32
            )
            s = jnp.where(allowed, s * scale, -1e30)
            top = jnp.max(s, axis=1, keepdims=True)
            e = jnp.exp(s - top)
            total = jnp.sum(e, axis=1, keepdims=True)
            o = jnp.dot(e.astype(BF), vbuf[...], preferred_element_type=F32) / total
            lse = top + jnp.log(total)
            lse_all = jnp.where(rlane == (2 * j + h) * 4 + rsub, lse, lse_all)
            halves_out.append(o.reshape(2 * zn, 8, HEAD))
        a, b = halves_out
        ra, rb = pltpu.roll(a, 4, 1), pltpu.roll(b, 4, 1)
        fsend[0, :, :, h * HEAD : (h + 1) * HEAD] = jnp.where(low8, a, rb).astype(BF)
        fsend[1, :, :, h * HEAD : (h + 1) * HEAD] = jnp.where(low8, ra, b).astype(BF)
    gather4 = (iota((pn, rows_all), 1) // 4 == iota((pn, rows_all), 0)).astype(F32)
    lses = jnp.dot(gather4, lse_all, preferred_element_type=F32, precision=HI)
    lsend[...] = lses.reshape(pn, 1, HEAD)

    def send_result(p):
        xx, zz = p // zn, p % zn
        remote(
            fsend.at[xx % 2, zz * 2 + xx // 2],
            frecv.at[wide],
            ais.at[2],
            air.at[2],
            {"wide": p, "narrow": nar},
        ).start()
        remote(
            lsend.at[zz * XS + xx], lrecv.at[wide], ais.at[3], air.at[3], {"wide": p, "narrow": nar}
        ).start()

    each_wide(send_result)
    own_far = pltpu.make_async_copy(fsend.at[jx, z * 2 + k], frecv.at[wide], loc.at[2])
    own_lse = pltpu.make_async_copy(lsend.at[z * XS + x], lrecv.at[wide], loc.at[3])
    own_far.start()
    own_lse.start()

    for i in range(2):
        took(hrecv.at[i], hr.at[i])
    key = hrecv[0, :, 2 * HEAD :].astype(F32)
    value = hrecv[1, :, 2 * HEAD :].astype(F32)
    key_first = jnp.concatenate([key[:reqs], key[:reqs]], axis=0)
    value_first = jnp.concatenate([value[:reqs], value[:reqs]], axis=0)
    second = iota((t_rows, 1), 0) >= reqs
    same, prev = [], []
    for g in range(4):
        q = hrecv[g // 2, :, (g % 2) * HEAD : (g % 2 + 1) * HEAD].astype(F32)
        same.append(jnp.sum(q * key, axis=1, keepdims=True) * scale)
        early = jnp.sum(q * key_first, axis=1, keepdims=True) * scale
        prev.append(jnp.where(second, early, -1e30))
    code = to_column(meta[0:1, :], t_rows)

    took(fsend.at[0, pl.ds(0, pn // 2)], ais.at[2])
    took(fsend.at[0, pl.ds(0, pn // 2 - 1)], ais.at[2])
    took(frecv.at[pl.ds(0, pn - 1)], air.at[2])
    took(lsend.at[pl.ds(0, pn - 1)], ais.at[3])
    took(lrecv.at[pl.ds(0, pn - 1)], air.at[3])
    own_far.wait()
    own_lse.wait()

    far_rows = frecv[...].astype(F32).reshape(8 * pn, 2 * HEAD).astype(BF)
    lse_rows = lrecv[...].reshape(pn, HEAD)
    owner_p = (iota((t_rows, pn), 1) == code // 8).astype(F32)
    lse_mine = jnp.dot(owner_p, lse_rows, preferred_element_type=F32, precision=HI)
    slot_cols = iota((t_rows, 8 * pn), 1)
    lane = iota((t_rows, HEAD), 1)
    for j in range(2):
        pickj = (slot_cols == code + 4 * j).astype(F32).astype(BF)
        far2 = jnp.dot(pickj, far_rows, preferred_element_type=F32)
        for h in range(2):
            g = 2 * j + h
            lse = jnp.sum(
                jnp.where(lane == g * 4 + code % 8, lse_mine, 0.0), axis=1, keepdims=True
            )
            top = jnp.maximum(jnp.maximum(lse, same[g]), prev[g])
            ef, es, ep = jnp.exp(lse - top), jnp.exp(same[g] - top), jnp.exp(prev[g] - top)
            total = ef + es + ep
            num = far2[:, h * HEAD : (h + 1) * HEAD] * ef + value * es + value_first * ep
            out[:, g * HEAD : (g + 1) * HEAD] = (num / total).astype(BF)

    for j in range(2):
        for part in range(2):
            sent(wx(j, part), selfcase & (jx == j))
    for o in range(XS):
        sent(tok1(o), selfcase) if o == 0 else tok1(o)[0].wait_send()
        sent(met1(o), selfcase) if o == 0 else met1(o)[0].wait_send()
    if zn > 1:
        took(wbuf.at[pl.ds(0, 2 * (zn - 1))], zs)
    took(wbuf.at[pl.ds(0, 2 * zn)], ps)
    if yn > 1:
        took(tokbuf.at[pl.ds(0, 2 * (yn - 1))], ys)
    for i in range(2):
        sent(home(i), selfcase & (jx == i))


def on_device(dims, tokens, qkv_weight, rotated_prefix_keys, shared_prefix_values, prefix_of, positions):
    zn, yn = dims
    pn = XS * zn
    reqs, _, feat = tokens.shape
    t_rows = reqs * STEPS
    depth = qkv_weight.shape[0]
    length = rotated_prefix_keys.shape[1]
    tok = tokens.transpose(1, 0, 2).reshape(t_rows, feat)
    vm = pl.BlockSpec(memory_space=pltpu.VMEM)
    hbm = pl.BlockSpec(memory_space=pl.ANY)
    dma = pltpu.SemaphoreType.DMA
    zmax, ymax = max(1, zn // 2), max(1, yn // 2)
    V = pltpu.VMEM
    result = pl.pallas_call(
        functools.partial(kernel, dims),
        out_shape=jax.ShapeDtypeStruct((t_rows, 4 * HEAD), BF),
        in_specs=[vm, hbm, hbm, hbm, vm, vm],
        out_specs=vm,
        scratch_shapes=[
            V((pn, depth, 3 * HEAD), BF),
            V((2 * yn, 2, t_rows, feat), BF),
            V((length, HEAD), BF),
            V((length, HEAD), BF),
            V((8, t_rows), I32),
            V((2, 2, 8, t_rows), I32),
            V((2, t_rows, HEAD), F32),
            V((2, t_rows, HEAD), F32),
            V((pn, 1, HEAD), F32),
            V((pn, 1, HEAD), F32),
            V((2, t_rows, 3 * HEAD), BF),
            V((2, t_rows, 3 * HEAD), BF),
            V((pn, 8, 2 * HEAD), BF),
            V((2 * zn, 2, 8, 2 * HEAD), BF),
            V((2, 2 * zn, 8, 2 * HEAD), BF),
            V((pn, 8, 2 * HEAD), BF),
            V((pn, 1, HEAD), F32),
            V((pn, 1, HEAD), F32),
            dma((2, 2)),
            dma((2, 2)),
            dma(()),
            dma((2, 2, zmax)),
            dma(()),
            dma(()),
            dma((XS,)),
            dma((2, 2)),
            dma((XS,)),
            dma((2, 2)),
            dma(()),
            dma((2, 2, 2, ymax)),
            dma((2,)),
            dma((2,)),
            dma((2,)),
            dma((4,)),
            dma((4,)),
            dma((4,)),
        ],
        compiler_params=pltpu.CompilerParams(
            collective_id=0, has_side_effects=True, vmem_limit_bytes=60 * 2**20
        ),
        name="decode_step",
    )(
        tok,
        qkv_weight,
        rotated_prefix_keys,
        shared_prefix_values,
        prefix_of.reshape(1, reqs),
        positions.reshape(1, reqs),
    )
    return result.reshape(STEPS, reqs, 4 * HEAD).transpose(1, 0, 2)


def solution(mesh):
    dims = (mesh.shape["wide"] // XS, mesh.shape["narrow"] // 2)
    return jax.shard_map(
        functools.partial(on_device, dims),
        mesh=mesh,
        in_specs=(
            P("wide", None, "narrow"),
            P("wide", "narrow"),
            P("wide", None, "narrow"),
            P("wide", None, "narrow"),
            P("wide", None),
            P("wide"),
        ),
        out_specs=P("wide", None, "narrow"),
        check_vma=False,
    )
```

time: 328 us -> 98.8 us (0.30)
  waiting for transfers between devices: 203 us -> 0 us
  Pallas kernels: 0 us -> 94 us
  starting transfers between devices: 55.9 us -> 0 us
  matrix products: 19.2 us -> 0 us
  local copies, waits for them, and re-layouts: 20.9 us -> 3.28 us
  between operations: 13.7 us -> 0.01 us
  other arithmetic: 11.4 us -> 0 us
    all_gather x2 -> x0, waiting for transfers between devices: 143 us -> none  [the longest x1 116 us: on_device(): lax.all_gather(qkv_weight, 'wide', axis=0, tiled=True)]
    pallas_call x0 -> x1, Pallas kernels: none -> 94 us  [on_device(): pl.pallas_call(functools.partial(kernel, dims), out_shape=jax.ShapeDtypeS...]
    all_to_all x5 -> x0, waiting for transfers between devices: 59.4 us -> none  [the longest x1 19.2 us: on_device(): lax.all_to_all(packed.reshape(owners, capacity, flat.shape[1]), 'wide', s...]
    all_to_all x5 -> x0, starting transfers between devices: 55.9 us -> none  [the longest x1 19.1 us: on_device(): lax.all_to_all(limits, 'wide', split_axis=0, concat_axis=0, tiled=True)]
    dot_general x6 -> x0, matrix products: 19.2 us -> none  [the longest x1 6.34 us: fold_rows(): return jnp.dot(inputs, piece, preferred_element_type=jnp.float32)]
    dot_general x1 -> x0, local copies, waits for them, and re-layouts: 10.6 us -> none  [fold_rows(): return jnp.dot(inputs, piece, preferred_element_type=jnp.float32)]
    reduce_sum x4 -> x0, other arithmetic: 6.42 us -> none  [the longest x1 4.57 us: prefix_part(): total = jnp.sum(weight, axis=-1)]
  transfers between devices with their start and end apart: 7 -> 0, of which waited for: 7 -> 0; matrix products, arithmetic and copies ran while one was open for 11% -> 0% of each run, Pallas kernels for 0% -> 0%
where the time goes in v1:
time: 98.8 us; the launch traced here: 97.3 us
  Pallas kernels  94 us (95%)
  local copies, waits for them, and re-layouts  3.28 us (3%)
    pallas_call x1, Pallas kernels, on_device(): pl.pallas_call(functools.partial(kernel, dims), out_shape=jax.ShapeDtypeS...  94 us

profile of v1, /device:TPU:1, one launch (start us, length us, event | category | flops | bytes accessed | tf_op | source)
XLA Modules:
  0.0 97.3 jit_solution(14015051618528063680)
XLA Ops:
  0.0 1.6 %copy.7 = bf16[2,64,640]{2,1,0:T(8,128)(2,1)} copy(bf16[2,64,640]{2,0,1:T(2,128)(2,1)} %bitcast.10) | data formatting | bytes 327680 | tf_op jit(solution)/shard_map/transpose | solution.py:505
  1.6 94.0 %decode_step.1 = bf16[128,512]{1,0:T(8,128)(2,1)} custom-call(bf16[128,640]{1,0:T(8,128)(2,1)} %bitcast.8, bf16[80,768]{1,0:T(8,128)(2,1)} %w.1, bf16[1,2048,128]{2,1,0:T(8,128)(2,1)} %keys.1, bf16[1,2048,128]{2,1,0:T(8,128)(2,1)} %vals.1, s32[1,64]{1,0:T(1,128)} %bitcast.11, s32[1,64]{1,0:T(1,128)} %bitcast.12), custom_call_target="tpu_custom_call" | custom-call | tf_op jit(solution)/shard_map/decode_step/pallas_call | solution.py:511
  95.6 1.7 %copy.10 = bf16[2,64,512]{2,0,1:T(2,128)(2,1)} copy(bf16[2,64,512]{2,1,0:T(8,128)(2,1)} %bitcast.9) | data formatting | bytes 262144 | tf_op jit(solution)/shard_map/reshape | solution.py:566

commit v2 on v1

v2 whole, which is shorter than its diff:
```python
import functools
import math

import jax
import jax.numpy as jnp
from jax import lax
from jax.experimental import pallas as pl
from jax.experimental.pallas import tpu as pltpu
from jax.sharding import PartitionSpec as P

HEAD = 128
STEPS = 2
XS = 4
PARTS = 3
XAT = 3
MESH = pl.DeviceIdType.MESH
BF = jnp.bfloat16
F32 = jnp.float32
I32 = jnp.int32
HI = lax.Precision.HIGHEST


def iota(shape, dim):
    return lax.broadcasted_iota(I32, shape, dim)


def to_column(row, n):
    eye = iota((n, row.shape[1]), 0) == iota((n, row.shape[1]), 1)
    return jnp.sum(jnp.where(eye, row, 0), axis=1, keepdims=True)


def frequencies():
    lane = iota((1, HEAD), 1) % (HEAD // 2)
    high, low = lane // 8, lane % 8
    a = jnp.full((1, HEAD), 1.0, F32)
    b = jnp.full((1, HEAD), 1.0, F32)
    for t in range(1, 8):
        a = jnp.where(high == t, 10000.0 ** (-8 * t / 64), a)
        b = jnp.where(low == t, 10000.0 ** (-t / 64), b)
    return a * b


def kernel(
    dims,
    traw,
    w,
    keys,
    vals,
    pref,
    pos,
    out,
    wown,
    tokin,
    tok,
    wbuf,
    tokbuf,
    kbuf,
    vbuf,
    meta,
    metabuf,
    cosbuf,
    sinbuf,
    limsend,
    limrecv,
    hsend,
    hrecv,
    qsend,
    qrecv,
    fsend,
    frecv,
    lsend,
    lrecv,
    wxs,
    wxr,
    zs,
    zr,
    ps,
    pr,
    t1s,
    t1r,
    m1s,
    m1r,
    xs,
    xr,
    xs2,
    xr2,
    kvs,
    hs,
    hr,
    qs,
    qr,
    qloc,
    fs,
    fr,
    floc,
    ais,
    air,
    loc,
):
    zn, yn = dims
    pn = XS * zn
    t_rows = tok.shape[0]
    reqs = t_rows // STEPS
    wide, nar = lax.axis_index("wide"), lax.axis_index("narrow")
    x, z = wide // zn, wide % zn
    y, c = nar // 2, nar % 2
    k, jx = x // 2, x % 2
    selfcase = k == c

    def dev(xx, zz, yy, cc):
        return {"wide": xx * zn + zz, "narrow": yy * 2 + cc}

    def remote(src, dst, ss, rs, where):
        return pltpu.make_async_remote_copy(
            src_ref=src, dst_ref=dst, send_sem=ss, recv_sem=rs, device_id=where, device_id_type=MESH
        )

    def took(ref, sem):
        pltpu.make_async_copy(ref, ref, sem).wait()

    up_z, down_z = (z + 1) % zn, (z + zn - 1) % zn

    barrier = pltpu.get_barrier_semaphore()
    peers = [dev((x + o) % XS, z, y, (c + d) % 2) for o in range(XS) for d in range(2) if o or d]
    if zn > 1:
        peers += [dev(x, up_z, y, c), dev(x, down_z, y, c)]
    if yn > 1:
        peers += [dev(x, z, (y + o) % yn, (c + d) % 2) for o in range(1, yn) for d in range(2)]
    for peer in peers:
        pl.semaphore_signal(barrier, inc=1, device_id=peer, device_id_type=MESH)

    kcopy = pltpu.make_async_copy(keys.at[0], kbuf, kvs.at[0])
    vcopy = pltpu.make_async_copy(vals.at[0], vbuf, kvs.at[1])
    kcopy.start()
    vcopy.start()

    wcopy = pltpu.make_async_copy(w, wown, loc.at[2])
    tcopy = pltpu.make_async_copy(traw, tokin, loc.at[3])
    wcopy.start()
    tcopy.start()
    wcopy.wait()
    pl.semaphore_wait(barrier, len(peers))

    def wx(j, part):
        start = 4 * HEAD + HEAD * j if part == 2 else HEAD * (2 * j + part)
        src = wown.at[:, pl.ds(start, HEAD)]
        dst = wbuf.at[part, wide]
        rsem = wxr.at[jx, part]
        return (
            lambda: remote(src, dst, wxs.at[j, part], rsem, dev(2 * c + j, z, y, k)),
            lambda: pltpu.make_async_copy(src, dst, rsem),
        )

    def either(pair, is_self):
        @pl.when(is_self)
        def _():
            pair[1]().start()

        @pl.when(jnp.logical_not(is_self))
        def _():
            pair[0]().start()

    def sent(pair, is_self):
        @pl.when(jnp.logical_not(is_self))
        def _():
            pair[0]().wait_send()

    for part in range(PARTS):
        for j in range(2):
            either(wx(j, part), selfcase & (jx == j))

    tcopy.wait()
    for step in range(STEPS):
        tok[step * reqs : (step + 1) * reqs] = tokin[:, step, :]

    def token(o):
        dst, rsem = tokbuf.at[nar, jx], t1r.at[nar]
        return (
            lambda: remote(tok, dst, t1s.at[o], rsem, dev(x, z, (y + o) % yn, k)),
            lambda: pltpu.make_async_copy(tok, dst, rsem),
        )

    yorder = [0, 1, 3, 2] if yn == 4 else list(range(yn))
    for o in yorder:
        if o:
            token(o)[0]().start()
        else:
            either(token(o), selfcase)

    pcol = to_column(pref[...], reqs)
    before = (pcol == pref[...]) & (iota((reqs, reqs), 0) < iota((reqs, reqs), 1))
    rank = jnp.sum(before.astype(I32), axis=0, keepdims=True)
    code_col = to_column(pref[...] * 8 + rank * 2, reqs)
    pos_col = to_column(pos[...], reqs)
    spread = iota((reqs, t_rows), 0) == iota((reqs, t_rows), 1) % reqs
    step_lane = iota((1, t_rows), 1) // reqs
    code_row = jnp.sum(jnp.where(spread, code_col, 0), axis=0, keepdims=True) + step_lane
    place_row = jnp.sum(jnp.where(spread, pos_col, 0), axis=0, keepdims=True) + step_lane
    which = iota((8, t_rows), 0)
    meta[...] = jnp.where(which == 0, code_row, jnp.where(which == 1, place_row, 0))


    def routes_to(o):
        dst, rsem = metabuf.at[c, jx], m1r.at[c, jx]
        return (
            lambda: remote(meta, dst, m1s.at[o], rsem, dev((x + o) % XS, z, y, k)),
            lambda: pltpu.make_async_copy(meta, dst, rsem),
        )

    for o in range(XS):
        if o:
            routes_to(o)[0]().start()
        else:
            either(routes_to(o), selfcase)

    near = jnp.where(selfcase, jx, 1 - jx)
    block = (near, 1 - near)

    def reach(n):
        return {(0, 0): n // 2, (0, 1): (n - 1) // 2, (1, 0): (n - 1) // 2, (1, 1): n // 2}

    zreach = reach(zn)
    zto = (up_z, down_z)

    def zslot(direction, a, d):
        origin = (z + zn - d) % zn if direction == 0 else (z + d) % zn
        return (2 * c + block[a]) * zn + origin

    def zsend(direction, a, part, d):
        ref = wbuf.at[part, zslot(direction, a, d)]
        remote(ref, ref, zs, zr.at[direction, a, part, d], dev(x, zto[direction], y, c)).start()

    def partner(direction, a, d):
        ref = wbuf.at[:, zslot(direction, a, d)]
        remote(ref, ref, ps, pr, dev(x, z, y, 1 - c)).start()

    order = [((y + o) % yn) * 2 + (c + cc) % 2 for o in yorder for cc in range(2)]
    plus = selfcase == (jx == 1)
    ahead = jnp.where(plus, (x + 1) % XS, (x + XS - 1) % XS)
    behind = jnp.where(plus, (x + XS - 1) % XS, (x + 1) % XS)
    onward = jnp.where(plus, 0, 1)

    def own_rows(m):
        @pl.when(selfcase)
        def _():
            ref = tokbuf.at[order[m], jx]
            took(ref, t1r.at[order[m]])
            for side in (1, XS - 1):
                remote(ref, ref, xs, xr.at[order[m]], dev((x + side) % XS, z, y, c)).start()

    def next_rows(m):
        ref = tokbuf.at[order[m], behind % 2]
        took(ref, xr.at[order[m]])

        @pl.when(order[m] % 2 == onward)
        def _():
            remote(ref, ref, xs2, xr2.at[order[m]], dev(ahead, z, y, c)).start()

    for a in range(2):
        for part in range(PARTS):
            took(wbuf.at[part, zslot(0, a, 0)], wxr.at[block[a], part])
            for direction in range(2):
                if zreach[direction, a] > 0:
                    zsend(direction, a, part, 0)
        partner(0, a, 0)
        for m in range(2):
            if 2 * a + m < 2 * yn:
                own_rows(2 * a + m)

    def angles():
        freq = frequencies()
        for i in range(2):
            for cc in range(2):
                took(metabuf.at[cc, i], m1r.at[cc, i])
            place = to_column(metabuf[0, i, 1:2, :], t_rows).astype(F32)
            angle = place * freq
            low = iota((t_rows, HEAD), 1) < HEAD // 2
            sine = jnp.sin(angle)
            cosbuf[i] = jnp.cos(angle)
            sinbuf[i] = jnp.where(low, -sine, sine)

    rest = list(range(4, 2 * yn))
    coming = list(range(2 * yn))
    for d in range(1, zn // 2 + 1):
        for part in range(PARTS):
            for a in range(2):
                for direction in range(2):
                    if d <= zreach[direction, a]:
                        took(
                            wbuf.at[part, zslot(direction, a, d)],
                            zr.at[direction, a, part, d - 1],
                        )
                        if d < zreach[direction, a]:
                            zsend(direction, a, part, d)
                        if part == PARTS - 1:
                            partner(direction, a, d)
        for m in rest[:2]:
            own_rows(m)
        rest = rest[2:]
        if d == 1:
            angles()
        if d >= XAT:
            for m in coming[:2]:
                next_rows(m)
            coming = coming[2:]
    for m in rest:
        own_rows(m)
    for m in coming:
        next_rows(m)

    @pl.when(jnp.logical_not(selfcase))
    def _():
        for m in range(2 * yn):
            took(tokbuf.at[order[m], 1 - behind % 2], xr2.at[order[m]])

    lane = iota((reqs, HEAD), 1)
    halves = jnp.where(lane < 4, pos_col // 64, pos_col % 64).astype(F32).astype(BF)
    code64 = pref[...] * 8 + rank * 2
    prow = iota((pn, reqs), 0) * 8
    lim = [
        jnp.dot(
            (code64 == prow + 2 * u).astype(F32).astype(BF), halves, preferred_element_type=F32
        )
        for u in range(2)
    ]
    limits = jnp.where((iota((pn, HEAD), 1) // 2) % 2 == 0, lim[0], lim[1])
    limsend[...] = limits.reshape(pn, 1, HEAD)

    took(wbuf.at[:, pl.ds(0, 2 * zn)], pr)

    def each_wide(fn):
        def step(o, carry):
            fn((wide + o) % pn)
            return carry

        lax.fori_loop(1, pn, step, 0)

    def send_limit(p):
        remote(
            limsend.at[p],
            limrecv.at[z * XS + x],
            ais.at[0],
            air.at[0],
            {"wide": p, "narrow": nar},
        ).start()

    each_wide(send_limit)
    own_limit = pltpu.make_async_copy(limsend.at[wide], limrecv.at[z * XS + x], loc.at[0])
    own_limit.start()

    nb = pn // (2 * yn)
    depth = w.shape[0]
    cosine = cosbuf[...].reshape(2 * t_rows, HEAD)
    sine = sinbuf[...].reshape(2 * t_rows, HEAD)

    def project(part):
        acc = None
        for n in range(2 * yn):
            left = tokbuf[n].reshape(2 * t_rows, tok.shape[1])
            right = wbuf[part, n * nb : (n + 1) * nb].reshape(nb * depth, HEAD)
            term = jnp.dot(left, right, preferred_element_type=F32)
            acc = term if acc is None else acc + term
        return acc

    def rotate(v):
        return v * cosine + pltpu.roll(v, HEAD // 2, 1) * sine

    codes = jnp.concatenate([metabuf[0, i, 0:1, :] + 4 * i for i in range(2)], axis=1)
    slots = iota((8 * pn, 2 * t_rows), 0)
    onehot = (slots == codes).astype(F32).astype(BF)
    for h in range(2):
        q = rotate(project(h)).astype(BF)
        packed = jnp.dot(onehot, q, preferred_element_type=F32)
        qsend[h] = packed.reshape(pn, 8, HEAD).astype(BF)

        def send_query(p, h=h):
            remote(
                qsend.at[h, p],
                qrecv.at[h, z * 2 + c, jx],
                qs.at[h],
                qr.at[h],
                {"wide": p, "narrow": y * 2 + k},
            ).start()

        each_wide(send_query)

        @pl.when(selfcase)
        def _():
            pltpu.make_async_copy(qsend.at[h, wide], qrecv.at[h, z * 2 + c, jx], qloc.at[h]).start()

        @pl.when(jnp.logical_not(selfcase))
        def _():
            send_query(wide)

        for i in range(2):
            hsend[i, :, h * HEAD : (h + 1) * HEAD] = q[i * t_rows : (i + 1) * t_rows]

    third = project(2)
    third = jnp.where(jx == 0, rotate(third), third).astype(BF)
    for i in range(2):
        hsend[i, :, 2 * HEAD :] = third[i * t_rows : (i + 1) * t_rows]

    def home(i):
        src, dst, rsem = hsend.at[i], hrecv.at[jx], hr.at[jx]
        return (
            lambda: remote(src, dst, hs.at[i], rsem, dev(2 * c + i, z, y, k)),
            lambda: pltpu.make_async_copy(src, dst, rsem),
        )

    for i in range(2):
        either(home(i), selfcase & (jx == i))

    kcopy.wait()
    vcopy.wait()
    took(limsend.at[pl.ds(0, pn - 1)], ais.at[0])
    took(limsend.at[pl.ds(0, pn - 1)], air.at[0])
    own_limit.wait()

    rows_all = 4 * pn
    lim_rows = limrecv[...].reshape(pn, HEAD).astype(BF)
    owner = (iota((rows_all, pn), 0) // 4 == iota((rows_all, pn), 1)).astype(F32).astype(BF)
    lim_all = jnp.dot(owner, lim_rows, preferred_element_type=F32)
    rlane, rsub = iota((rows_all, HEAD), 1), iota((rows_all, HEAD), 0) % 4
    pick = jnp.where(rlane == rsub, 64.0, jnp.where(rlane == rsub + 4, 1.0, 0.0))
    limit = jnp.sum(lim_all * pick, axis=1, keepdims=True).astype(I32)

    scale = 1.0 / HEAD**0.5
    length = kbuf.shape[0]
    allowed = iota((rows_all, length), 1) < limit
    lse_all = jnp.zeros((rows_all, HEAD), F32)
    low8 = iota((2 * zn, 8, HEAD), 1) < 4
    gather4 = (iota((pn, rows_all), 1) // 4 == iota((pn, rows_all), 0)).astype(F32)

    def own_result(h):
        return pltpu.make_async_copy(fsend.at[h, jx, z * 2 + k], frecv.at[h, wide], floc.at[h])

    own_lse = pltpu.make_async_copy(lsend.at[z * XS + x], lrecv.at[wide], loc.at[1])
    for h in range(2):

        @pl.when(selfcase)
        def _():
            pltpu.make_async_copy(qsend.at[h, wide], qrecv.at[h, z * 2 + c, jx], qloc.at[h]).wait()
            took(qsend.at[h, pl.ds(0, pn - 1)], qs.at[h])
            took(qsend.at[h, pl.ds(0, pn - 1)], qr.at[h])

        @pl.when(jnp.logical_not(selfcase))
        def _():
            took(qsend.at[h], qs.at[h])
            took(qsend.at[h], qr.at[h])

        halves_out = []
        for j in range(2):
            q = qrecv[h, :, j].astype(F32).reshape(rows_all, HEAD).astype(BF)
            s = lax.dot_general(
                q, kbuf[...], (((1,), (1,)), ((), ())), preferred_element_type=F32
            )
            s = jnp.where(allowed, s * scale, -1e30)
            top = jnp.max(s, axis=1, keepdims=True)
            e = jnp.exp(s - top)
            total = jnp.sum(e, axis=1, keepdims=True)
            o = jnp.dot(e.astype(BF), vbuf[...], preferred_element_type=F32) / total
            lse = top + jnp.log(total)
            lse_all = jnp.where(rlane == (2 * j + h) * 4 + rsub, lse, lse_all)
            halves_out.append(o.reshape(2 * zn, 8, HEAD))
        a, b = halves_out
        ra, rb = pltpu.roll(a, 4, 1), pltpu.roll(b, 4, 1)
        fsend[h, 0] = jnp.where(low8, a, rb).astype(BF)
        fsend[h, 1] = jnp.where(low8, ra, b).astype(BF)
        if h == 1:
            lses = jnp.dot(gather4, lse_all, preferred_element_type=F32, precision=HI)
            lsend[...] = lses.reshape(pn, 1, HEAD)

        def send_result(p, h=h):
            xx, zz = p // zn, p % zn
            where = {"wide": p, "narrow": nar}
            if h == 1:
                remote(lsend.at[zz * XS + xx], lrecv.at[wide], ais.at[1], air.at[1], where).start()
            remote(
                fsend.at[h, xx % 2, zz * 2 + xx // 2], frecv.at[h, wide], fs.at[h], fr.at[h], where
            ).start()

        each_wide(send_result)
        own_result(h).start()
    own_lse.start()

    for i in range(2):
        took(hrecv.at[i], hr.at[i])
    key = hrecv[0, :, 2 * HEAD :].astype(F32)
    value = hrecv[1, :, 2 * HEAD :].astype(F32)
    key_first = jnp.concatenate([key[:reqs], key[:reqs]], axis=0)
    value_first = jnp.concatenate([value[:reqs], value[:reqs]], axis=0)
    second = iota((t_rows, 1), 0) >= reqs
    same, prev = [], []
    for g in range(4):
        q = hrecv[g // 2, :, (g % 2) * HEAD : (g % 2 + 1) * HEAD].astype(F32)
        same.append(jnp.sum(q * key, axis=1, keepdims=True) * scale)
        early = jnp.sum(q * key_first, axis=1, keepdims=True) * scale
        prev.append(jnp.where(second, early, -1e30))
    code = to_column(meta[0:1, :], t_rows)

    for h in range(2):
        took(frecv.at[h, pl.ds(0, pn - 1)], fs.at[h])
        took(frecv.at[h, pl.ds(0, pn - 1)], fr.at[h])
        own_result(h).wait()
    took(lsend.at[pl.ds(0, pn - 1)], ais.at[1])
    took(lrecv.at[pl.ds(0, pn - 1)], air.at[1])
    own_lse.wait()

    far_rows = [frecv[h].astype(F32).reshape(8 * pn, HEAD).astype(BF) for h in range(2)]
    lse_rows = lrecv[...].reshape(pn, HEAD)
    owner_p = (iota((t_rows, pn), 1) == code // 8).astype(F32)
    lse_mine = jnp.dot(owner_p, lse_rows, preferred_element_type=F32, precision=HI)
    slot_cols = iota((t_rows, 8 * pn), 1)
    lane = iota((t_rows, HEAD), 1)
    for j in range(2):
        pickj = (slot_cols == code + 4 * j).astype(F32).astype(BF)
        for h in range(2):
            far = jnp.dot(pickj, far_rows[h], preferred_element_type=F32)
            g = 2 * j + h
            lse = jnp.sum(
                jnp.where(lane == g * 4 + code % 8, lse_mine, 0.0), axis=1, keepdims=True
            )
            top = jnp.maximum(jnp.maximum(lse, same[g]), prev[g])
            ef, es, ep = jnp.exp(lse - top), jnp.exp(same[g] - top), jnp.exp(prev[g] - top)
            total = ef + es + ep
            num = far * ef + value * es + value_first * ep
            out[:, g * HEAD : (g + 1) * HEAD] = (num / total).astype(BF)

    for j in range(2):
        for part in range(PARTS):
            sent(wx(j, part), selfcase & (jx == j))
    for o in range(XS):
        if o:
            routes_to(o)[0]().wait_send()
        else:
            sent(routes_to(o), selfcase)
    for o in yorder:
        if o:
            token(o)[0]().wait_send()
        else:
            sent(token(o), selfcase)

    @pl.when(selfcase)
    def _():
        took(tokbuf, xs)

    took(tokbuf.at[pl.ds(0, yn), 0], xs2)
    if zn > 1:
        took(wbuf.at[:, pl.ds(0, 2 * (zn - 1))], zs)
    took(wbuf.at[:, pl.ds(0, 2 * zn)], ps)
    for i in range(2):
        sent(home(i), selfcase & (jx == i))


def on_device(dims, tokens, qkv_weight, rotated_prefix_keys, shared_prefix_values, prefix_of, positions):
    zn, yn = dims
    pn = XS * zn
    reqs, _, feat = tokens.shape
    t_rows = reqs * STEPS
    depth = qkv_weight.shape[0]
    length = rotated_prefix_keys.shape[1]
    vm = pl.BlockSpec(memory_space=pltpu.VMEM)
    hbm = pl.BlockSpec(memory_space=pl.ANY)
    dma = pltpu.SemaphoreType.DMA
    zmax = max(1, zn // 2)
    V = pltpu.VMEM
    result = pl.pallas_call(
        functools.partial(kernel, dims),
        out_shape=jax.ShapeDtypeStruct((t_rows, 4 * HEAD), BF),
        in_specs=[hbm, hbm, hbm, hbm, vm, vm],
        out_specs=vm,
        scratch_shapes=[
            V((depth, 6 * HEAD), BF),
            V((reqs, STEPS, feat), BF),
            V((t_rows, feat), BF),
            V((PARTS, pn, depth, HEAD), BF),
            V((2 * yn, 2, t_rows, feat), BF),
            V((length, HEAD), BF),
            V((length, HEAD), BF),
            V((8, t_rows), I32),
            V((2, 2, 8, t_rows), I32),
            V((2, t_rows, HEAD), F32),
            V((2, t_rows, HEAD), F32),
            V((pn, 1, HEAD), F32),
            V((pn, 1, HEAD), F32),
            V((2, t_rows, 3 * HEAD), BF),
            V((2, t_rows, 3 * HEAD), BF),
            V((2, pn, 8, HEAD), BF),
            V((2, 2 * zn, 2, 8, HEAD), BF),
            V((2, 2, 2 * zn, 8, HEAD), BF),
            V((2, pn, 8, HEAD), BF),
            V((pn, 1, HEAD), F32),
            V((pn, 1, HEAD), F32),
            dma((2, PARTS)),
            dma((2, PARTS)),
            dma(()),
            dma((2, 2, PARTS, zmax)),
            dma(()),
            dma(()),
            dma((yn,)),
            dma((2 * yn,)),
            dma((XS,)),
            dma((2, 2)),
            dma(()),
            dma((2 * yn,)),
            dma(()),
            dma((2 * yn,)),
            *[dma((2,)) for _ in range(11)],
            dma((4,)),
        ],
        compiler_params=pltpu.CompilerParams(
            collective_id=0, has_side_effects=True, vmem_limit_bytes=60 * 2**20
        ),
        name="decode_step",
    )(
        tokens,
        qkv_weight,
        rotated_prefix_keys,
        shared_prefix_values,
        prefix_of.reshape(1, reqs),
        positions.reshape(1, reqs),
    )
    return result.reshape(STEPS, reqs, 4 * HEAD).transpose(1, 0, 2)


def solution(mesh):
    dims = (mesh.shape["wide"] // XS, mesh.shape["narrow"] // 2)
    return jax.shard_map(
        functools.partial(on_device, dims),
        mesh=mesh,
        in_specs=(
            P("wide", None, "narrow"),
            P("wide", "narrow"),
            P("wide", None, "narrow"),
            P("wide", None, "narrow"),
            P("wide", None),
            P("wide"),
        ),
        out_specs=P("wide", None, "narrow"),
        check_vma=False,
    )
```

time: 98.8 us -> 83 us (0.84); the launches traced: 97.3 us -> 82.8 us
  Pallas kernels: 94 us -> 81.1 us
  local copies, waits for them, and re-layouts: 3.28 us -> 1.7 us
    pallas_call x1, Pallas kernels: 94 us -> 81.1 us  [on_device(): pl.pallas_call(functools.partial(kernel, dims), out_shape=jax.ShapeDtypeS...]
    transpose x1 -> x0, local copies, waits for them, and re-layouts: 1.59 us -> none  [on_device(): tok = tokens.transpose(1, 0, 2).reshape(t_rows, feat)]
where the time goes in v2:
time: 83 us; the launch traced here: 82.8 us
  Pallas kernels  81.1 us (98%)
  local copies, waits for them, and re-layouts  1.7 us (2%)
    pallas_call x1, Pallas kernels, on_device(): pl.pallas_call(functools.partial(kernel, dims), out_shape=jax.ShapeDtypeS...  81.1 us
    reshape x1, local copies, waits for them, and re-layouts, on_device(): return result.reshape(STEPS, reqs, 4 * HEAD).transpose(1, 0, 2)  1.7 us

profile of v2, /device:TPU:1, one launch (start us, length us, event | category | flops | bytes accessed | tf_op | source)
XLA Modules:
  0.0 82.8 jit_solution(17099637271159753057)
XLA Ops:
  0.0 81.1 %decode_step.1 = bf16[128,512]{1,0:T(8,128)(2,1)} custom-call(bf16[64,2,640]{2,1,0:T(2,128)(2,1)} %traw.1, bf16[80,768]{1,0:T(8,128)(2,1)} %w.1, bf16[1,2048,128]{2,1,0:T(8,128)(2,1)} %keys.1, bf16[1,2048,128]{2,1,0:T(8,128)(2,1)} %vals.1, s32[1,64]{1,0:T(1,128)} %bitcast.7, s32[1,64]{1,0:T(1,128)} %bitcast.8), custom_call_target="tpu_custom_call" | custom-call | tf_op jit(solution)/shard_map/decode_step/pallas_call | solution.py:567
  81.1 1.7 %copy.9 = bf16[2,64,512]{2,0,1:T(2,128)(2,1)} copy(bf16[2,64,512]{2,1,0:T(8,128)(2,1)} %bitcast.6) | data formatting | bytes 262144 | tf_op jit(solution)/shard_map/reshape | solution.py:623

commit v3 on v2

--- a/solution.py
+++ b/solution.py
@@ -213,6 +213,33 @@
         else:
             either(routes_to(o), selfcase)
 
+    lane = iota((reqs, HEAD), 1)
+    halves = jnp.where(lane < 4, pos_col // 64, pos_col % 64).astype(F32).astype(BF)
+    code64 = pref[...] * 8 + rank * 2
+    prow = iota((pn, reqs), 0) * 8
+    lim = [
+        jnp.dot(
+            (code64 == prow + 2 * u).astype(F32).astype(BF), halves, preferred_element_type=F32
+        )
+        for u in range(2)
+    ]
+    limits = jnp.where((iota((pn, HEAD), 1) // 2) % 2 == 0, lim[0], lim[1])
+    limsend[...] = limits.reshape(pn, 1, HEAD)
+
+    def send_limit(xx, zz):
+        remote(
+            limsend.at[xx * zn + zz],
+            limrecv.at[z * XS + x],
+            ais.at[0],
+            air.at[0],
+            dev(xx, zz, y, c),
+        ).start()
+
+    own_limit = pltpu.make_async_copy(limsend.at[wide], limrecv.at[z * XS + x], loc.at[0])
+    own_limit.start()
+    for o in range(1, XS):
+        send_limit((x + o) % XS, z)
+
     near = jnp.where(selfcase, jx, 1 - jx)
     block = (near, 1 - near)
 
@@ -230,9 +257,9 @@
         ref = wbuf.at[part, zslot(direction, a, d)]
         remote(ref, ref, zs, zr.at[direction, a, part, d], dev(x, zto[direction], y, c)).start()
 
-    def partner(direction, a, d):
-        ref = wbuf.at[:, zslot(direction, a, d)]
-        remote(ref, ref, ps, pr, dev(x, z, y, 1 - c)).start()
+    def partner(direction, a, part, d):
+        ref = wbuf.at[part, zslot(direction, a, d)]
+        remote(ref, ref, ps, pr.at[part], dev(x, z, y, 1 - c)).start()
 
     order = [((y + o) % yn) * 2 + (c + cc) % 2 for o in yorder for cc in range(2)]
     plus = selfcase == (jx == 1)
@@ -262,7 +289,7 @@
             for direction in range(2):
                 if zreach[direction, a] > 0:
                     zsend(direction, a, part, 0)
-        partner(0, a, 0)
+            partner(0, a, part, 0)
         for m in range(2):
             if 2 * a + m < 2 * yn:
                 own_rows(2 * a + m)
@@ -281,19 +308,28 @@
 
     rest = list(range(4, 2 * yn))
     coming = list(range(2 * yn))
-    for d in range(1, zn // 2 + 1):
+
+    def ring(d, part):
+        for a in range(2):
+            for direction in range(2):
+                if d <= zreach[direction, a]:
+                    took(
+                        wbuf.at[part, zslot(direction, a, d)],
+                        zr.at[direction, a, part, d - 1],
+                    )
+                    if d < zreach[direction, a]:
+                        zsend(direction, a, part, d)
+                    partner(direction, a, part, d)
+
+    last = zn // 2
+    for d in range(1, last + 1):
         for part in range(PARTS):
-            for a in range(2):
-                for direction in range(2):
-                    if d <= zreach[direction, a]:
-                        took(
-                            wbuf.at[part, zslot(direction, a, d)],
-                            zr.at[direction, a, part, d - 1],
-                        )
-                        if d < zreach[direction, a]:
-                            zsend(direction, a, part, d)
-                        if part == PARTS - 1:
-                            partner(direction, a, d)
+            if d < last or part == 0:
+                ring(d, part)
+        for o in range(XS):
+            send_limit((x + o) % XS, (z + zn - d) % zn)
+            if d <= (zn - 1) // 2:
+                send_limit((x + o) % XS, (z + d) % zn)
         for m in rest[:2]:
             own_rows(m)
         rest = rest[2:]
@@ -313,40 +349,17 @@
         for m in range(2 * yn):
             took(tokbuf.at[order[m], 1 - behind % 2], xr2.at[order[m]])
 
-    lane = iota((reqs, HEAD), 1)
-    halves = jnp.where(lane < 4, pos_col // 64, pos_col % 64).astype(F32).astype(BF)
-    code64 = pref[...] * 8 + rank * 2
-    prow = iota((pn, reqs), 0) * 8
-    lim = [
-        jnp.dot(
-            (code64 == prow + 2 * u).astype(F32).astype(BF), halves, preferred_element_type=F32
-        )
-        for u in range(2)
-    ]
-    limits = jnp.where((iota((pn, HEAD), 1) // 2) % 2 == 0, lim[0], lim[1])
-    limsend[...] = limits.reshape(pn, 1, HEAD)
-
-    took(wbuf.at[:, pl.ds(0, 2 * zn)], pr)
-
     def each_wide(fn):
-        def step(o, carry):
-            fn((wide + o) % pn)
+        half = zn // 2
+
+        def step(t, carry):
+            lap = t // XS
+            away = half - (lap + 1) // 2
+            dz = jnp.where(lap % 2 == 1, away, (zn - away) % zn)
+            fn(((x + t + 1) % XS) * zn + (z + dz) % zn)
             return carry
 
-        lax.fori_loop(1, pn, step, 0)
-
-    def send_limit(p):
-        remote(
-            limsend.at[p],
-            limrecv.at[z * XS + x],
-            ais.at[0],
-            air.at[0],
-            {"wide": p, "narrow": nar},
-        ).start()
-
-    each_wide(send_limit)
-    own_limit = pltpu.make_async_copy(limsend.at[wide], limrecv.at[z * XS + x], loc.at[0])
-    own_limit.start()
+        lax.fori_loop(0, pn - 1, step, 0)
 
     nb = pn // (2 * yn)
     depth = w.shape[0]
@@ -369,6 +382,10 @@
     slots = iota((8 * pn, 2 * t_rows), 0)
     onehot = (slots == codes).astype(F32).astype(BF)
     for h in range(2):
+        if h and last:
+            for part in range(1, PARTS):
+                ring(last, part)
+        took(wbuf.at[h, pl.ds(0, 2 * zn)], pr.at[h])
         q = rotate(project(h)).astype(BF)
         packed = jnp.dot(onehot, q, preferred_element_type=F32)
         qsend[h] = packed.reshape(pn, 8, HEAD).astype(BF)
@@ -395,6 +412,7 @@
         for i in range(2):
             hsend[i, :, h * HEAD : (h + 1) * HEAD] = q[i * t_rows : (i + 1) * t_rows]
 
+    took(wbuf.at[2, pl.ds(0, 2 * zn)], pr.at[2])
     third = project(2)
     third = jnp.where(jx == 0, rotate(third), third).astype(BF)
     for i in range(2):
@@ -596,7 +614,7 @@
             dma(()),
             dma((2, 2, PARTS, zmax)),
             dma(()),
-            dma(()),
+            dma((PARTS,)),
             dma((yn,)),
             dma((2 * yn,)),
             dma((XS,)),

time: 83 us -> 79.2 us (0.954)
  Pallas kernels: 81.1 us -> 77.4 us
    pallas_call x1, Pallas kernels: 81.1 us -> 77.4 us  [on_device(): pl.pallas_call(functools.partial(kernel, dims), out_shape=jax.ShapeDtypeS...]
where the time goes in v3:
time: 79.2 us; the launch traced here: 79.1 us
  Pallas kernels  77.4 us (98%)
  local copies, waits for them, and re-layouts  1.7 us (2%)
    pallas_call x1, Pallas kernels, on_device(): pl.pallas_call(functools.partial(kernel, dims), out_shape=jax.ShapeDtypeS...  77.4 us
    reshape x1, local copies, waits for them, and re-layouts, on_device(): return result.reshape(STEPS, reqs, 4 * HEAD).transpose(1, 0, 2)  1.7 us

profile of v3, /device:TPU:1, one launch (start us, length us, event | category | flops | bytes accessed | tf_op | source)
XLA Modules:
  0.0 79.1 jit_solution(4885894615276291030)
XLA Ops:
  0.0 77.4 %decode_step.1 = bf16[128,512]{1,0:T(8,128)(2,1)} custom-call(bf16[64,2,640]{2,1,0:T(2,128)(2,1)} %traw.1, bf16[80,768]{1,0:T(8,128)(2,1)} %w.1, bf16[1,2048,128]{2,1,0:T(8,128)(2,1)} %keys.1, bf16[1,2048,128]{2,1,0:T(8,128)(2,1)} %vals.1, s32[1,64]{1,0:T(1,128)} %bitcast.7, s32[1,64]{1,0:T(1,128)} %bitcast.8), custom_call_target="tpu_custom_call" | custom-call | tf_op jit(solution)/shard_map/decode_step/pallas_call | solution.py:585
  77.4 1.7 %copy.9 = bf16[2,64,512]{2,0,1:T(2,128)(2,1)} copy(bf16[2,64,512]{2,1,0:T(8,128)(2,1)} %bitcast.6) | data formatting | bytes 262144 | tf_op jit(solution)/shard_map/reshape | solution.py:641

commit v4 on v3

--- a/solution.py
+++ b/solution.py
@@ -49,7 +49,6 @@
     pref,
     pos,
     out,
-    wown,
     tokin,
     tok,
     wbuf,
@@ -70,6 +69,7 @@
     frecv,
     lsend,
     lrecv,
+    farbuf,
     wxs,
     wxr,
     zs,
@@ -134,16 +134,13 @@
     kcopy.start()
     vcopy.start()
 
-    wcopy = pltpu.make_async_copy(w, wown, loc.at[2])
     tcopy = pltpu.make_async_copy(traw, tokin, loc.at[3])
-    wcopy.start()
     tcopy.start()
-    wcopy.wait()
     pl.semaphore_wait(barrier, len(peers))
 
     def wx(j, part):
         start = 4 * HEAD + HEAD * j if part == 2 else HEAD * (2 * j + part)
-        src = wown.at[:, pl.ds(start, HEAD)]
+        src = w.at[:, pl.ds(start, HEAD)]
         dst = wbuf.at[part, wide]
         rsem = wxr.at[jx, part]
         return (
@@ -246,7 +243,7 @@
     def reach(n):
         return {(0, 0): n // 2, (0, 1): (n - 1) // 2, (1, 0): (n - 1) // 2, (1, 1): n // 2}
 
-    zreach = reach(zn)
+    zreach, last = reach(zn), zn // 2
     zto = (up_z, down_z)
 
     def zslot(direction, a, d):
@@ -256,6 +253,8 @@
     def zsend(direction, a, part, d):
         ref = wbuf.at[part, zslot(direction, a, d)]
         remote(ref, ref, zs, zr.at[direction, a, part, d], dev(x, zto[direction], y, c)).start()
+        if d + 1 == last > 1:
+            remote(ref, ref, ps, pr.at[part], dev(x, zto[direction], y, 1 - c)).start()
 
     def partner(direction, a, part, d):
         ref = wbuf.at[part, zslot(direction, a, d)]
@@ -319,9 +318,9 @@
                     )
                     if d < zreach[direction, a]:
                         zsend(direction, a, part, d)
-                    partner(direction, a, part, d)
-
-    last = zn // 2
+                    if d < last or last == 1:
+                        partner(direction, a, part, d)
+
     for d in range(1, last + 1):
         for part in range(PARTS):
             if d < last or part == 0:
@@ -516,33 +515,30 @@
         prev.append(jnp.where(second, early, -1e30))
     code = to_column(meta[0:1, :], t_rows)
 
+    owner_p = (iota((t_rows, pn), 1) == code // 8).astype(F32)
+    slot_cols = iota((t_rows, 8 * pn), 1)
+    lane = iota((t_rows, HEAD), 1)
+    picks = [(slot_cols == code + 4 * j).astype(F32).astype(BF) for j in range(2)]
     for h in range(2):
         took(frecv.at[h, pl.ds(0, pn - 1)], fs.at[h])
         took(frecv.at[h, pl.ds(0, pn - 1)], fr.at[h])
         own_result(h).wait()
+        far_rows = frecv[h].astype(F32).reshape(8 * pn, HEAD).astype(BF)
+        for j in range(2):
+            farbuf[2 * j + h] = jnp.dot(picks[j], far_rows, preferred_element_type=F32)
     took(lsend.at[pl.ds(0, pn - 1)], ais.at[1])
     took(lrecv.at[pl.ds(0, pn - 1)], air.at[1])
     own_lse.wait()
 
-    far_rows = [frecv[h].astype(F32).reshape(8 * pn, HEAD).astype(BF) for h in range(2)]
     lse_rows = lrecv[...].reshape(pn, HEAD)
-    owner_p = (iota((t_rows, pn), 1) == code // 8).astype(F32)
     lse_mine = jnp.dot(owner_p, lse_rows, preferred_element_type=F32, precision=HI)
-    slot_cols = iota((t_rows, 8 * pn), 1)
-    lane = iota((t_rows, HEAD), 1)
-    for j in range(2):
-        pickj = (slot_cols == code + 4 * j).astype(F32).astype(BF)
-        for h in range(2):
-            far = jnp.dot(pickj, far_rows[h], preferred_element_type=F32)
-            g = 2 * j + h
-            lse = jnp.sum(
-                jnp.where(lane == g * 4 + code % 8, lse_mine, 0.0), axis=1, keepdims=True
-            )
-            top = jnp.maximum(jnp.maximum(lse, same[g]), prev[g])
-            ef, es, ep = jnp.exp(lse - top), jnp.exp(same[g] - top), jnp.exp(prev[g] - top)
-            total = ef + es + ep
-            num = far * ef + value * es + value_first * ep
-            out[:, g * HEAD : (g + 1) * HEAD] = (num / total).astype(BF)
+    for g in range(4):
+        lse = jnp.sum(jnp.where(lane == g * 4 + code % 8, lse_mine, 0.0), axis=1, keepdims=True)
+        top = jnp.maximum(jnp.maximum(lse, same[g]), prev[g])
+        ef, es, ep = jnp.exp(lse - top), jnp.exp(same[g] - top), jnp.exp(prev[g] - top)
+        total = ef + es + ep
+        num = farbuf[g] * ef + value * es + value_first * ep
+        out[:, g * HEAD : (g + 1) * HEAD] = (num / total).astype(BF)
 
     for j in range(2):
         for part in range(PARTS):
@@ -584,11 +580,10 @@
     V = pltpu.VMEM
     result = pl.pallas_call(
         functools.partial(kernel, dims),
-        out_shape=jax.ShapeDtypeStruct((t_rows, 4 * HEAD), BF),
+        out_shape=V((t_rows, 4 * HEAD), BF),
         in_specs=[hbm, hbm, hbm, hbm, vm, vm],
         out_specs=vm,
         scratch_shapes=[
-            V((depth, 6 * HEAD), BF),
             V((reqs, STEPS, feat), BF),
             V((t_rows, feat), BF),
             V((PARTS, pn, depth, HEAD), BF),
@@ -609,6 +604,7 @@
             V((2, pn, 8, HEAD), BF),
             V((pn, 1, HEAD), F32),
             V((pn, 1, HEAD), F32),
+            V((4, t_rows, HEAD), F32),
             dma((2, PARTS)),
             dma((2, PARTS)),
             dma(()),

time: 79.2 us -> 77.3 us (0.976)
  Pallas kernels: 77.4 us -> 76.4 us
  local copies, waits for them, and re-layouts: 1.7 us -> 0.79 us
    pallas_call x1, Pallas kernels: 77.4 us -> 76.4 us  [on_device(): pl.pallas_call(functools.partial(kernel, dims), out_shape=V((t_rows, 4 *...]
    reshape x1, local copies, waits for them, and re-layouts: 1.7 us -> 0.79 us  [on_device(): return result.reshape(STEPS, reqs, 4 * HEAD).transpose(1, 0, 2)]
where the time goes in v4:
time: 77.3 us; the launch traced here: 77.2 us
  Pallas kernels  76.4 us (99%)
  local copies, waits for them, and re-layouts  0.79 us (1%)
    pallas_call x1, Pallas kernels, on_device(): pl.pallas_call(functools.partial(kernel, dims), out_shape=V((t_rows, 4 *...  76.4 us

profile of v4, /device:TPU:1, one launch (start us, length us, event | category | flops | bytes accessed | tf_op | source)
XLA Modules:
  0.0 77.2 jit_solution(14363577620890817964)
XLA Ops:
  0.0 76.4 %decode_step.1 = bf16[128,512]{1,0:T(8,128)(2,1)S(1)} custom-call(bf16[64,2,640]{2,1,0:T(2,128)(2,1)} %traw.1, bf16[80,768]{1,0:T(8,128)(2,1)} %w.1, bf16[1,2048,128]{2,1,0:T(8,128)(2,1)} %keys.1, bf16[1,2048,128]{2,1,0:T(8,128)(2,1)} %vals.1, s32[1,64]{1,0:T(1,128)} %bitcast.7, s32[1,64]{1,0:T(1,128)} %bitcast.8), custom_call_target="tpu_custom_call" | custom-call | tf_op jit(solution)/shard_map/decode_step/pallas_call | solution.py:581
  76.4 0.8 %copy.9 = bf16[2,64,512]{2,0,1:T(2,128)(2,1)} copy(bf16[2,64,512]{2,1,0:T(8,128)(2,1)S(1)} %bitcast.6) | data formatting | bytes 262144 | tf_op jit(solution)/shard_map/reshape | solution.py:637
